TPU v7x, 256 devices: a whole 4x4x8 slice. The times are simulated.
256 devices in a mesh: width: 16 (over z, x_hi), chan: 16 (over y, x_lo, core).
Axes of the slice: x: 4 (x_hi: 2, x_lo: 2; x = x_hi * 2 + x_lo), y: 4, z: 8, core: 2. Of those that a mesh axis runs over, the one named last changes fastest.
Arguments:
- activations: bfloat16 [512, 2, 12288], P('chan', None, 'width'), may hold values from -6 to 6
- filters: bfloat16 [512, 3, 3, 512], P('chan'), may hold values from -0.125 to 0.125
- cotangent: bfloat16 [512, 2, 12288], P('chan', None, 'width'), may hold values from -6 to 6
Outputs:
- conv_output: bfloat16 [512, 2, 12288], P('chan', None, 'width')
- input_grad: bfloat16 [512, 2, 12288], P('chan', None, 'width')
- filter_grad: float32 [512, 3, 3, 512], P('chan')
All inputs are finite; a program needn't handle non-finite values.
Results may differ from a plain program's by a relative error of at most 0.001.
Values may be sent and summed in bfloat16 or wider, within the bound.
A program may use at most 128 MiB of HBM per device.

v0:
```python
import math
import jax
import jax.numpy as jnp
from jax import lax
from jax.sharding import PartitionSpec as P


def padded_2(shard, sides, width):
    for axis, dim in sides:
        devices, length = (lax.axis_size(axis), shard.shape[dim])
        up = [(i, (i + 1) % devices) for i in range(devices - 1)]
        down = [(j, i) for i, j in up]
        last = lax.slice_in_dim(shard, length - width, length, axis=dim)
        leading = lax.slice_in_dim(shard, 0, width, axis=dim)
        before = lax.ppermute(last, axis, up)
        after = lax.ppermute(leading, axis, down)
        shard = jnp.concatenate([before, shard, after], axis=dim)
    return shard


def pad_rows(field):
    return jnp.pad(field, ((0, 0), (1, 1), (0, 0)))


def stack_taps(padded, rows, cols, flipped):
    pieces = []
    for tap_row in range(3):
        for tap_col in range(3):
            first_row = 2 - tap_row if flipped else tap_row
            first_col = 2 - tap_col if flipped else tap_col
            pieces.append(
                padded[:, first_row : first_row + rows, first_col : first_col + cols].reshape(
                    padded.shape[0], rows * cols
                )
            )
    return jnp.concatenate(pieces, 0)


def tap_major(block):
    number_in = block.shape[0]
    number_out = block.shape[3]
    return jnp.transpose(block, (1, 2, 0, 3)).reshape(9 * number_in, number_out)


def body(activations, filters, cotangent):
    cin_dev, rows, cols = activations.shape
    cout_dev = cotangent.shape[0]
    edged = padded_2(activations, (("width", 2),), 1)
    source_stack = stack_taps(pad_rows(edged), rows, cols, False)
    block = tap_major(filters)
    summed = lax.dot_general(
        block, source_stack, (((0,), (0,)), ((), ())), preferred_element_type=jnp.float32
    )
    forward = lax.psum_scatter(
        summed.reshape(cout_dev * lax.axis_size("chan"), rows, cols),
        "chan",
        scatter_dimension=0,
        tiled=True,
    )
    conv_output = forward.astype(jnp.bfloat16)
    grad_edged = padded_2(cotangent, (("width", 2),), 1)
    shards = lax.all_gather(grad_edged, "chan", axis=0, tiled=True)
    number_rows = shards.shape[0]
    block = filters.reshape(cin_dev, 9 * number_rows)
    grad_stack = stack_taps(pad_rows(shards), rows, cols, True)
    input_sum = jnp.dot(block, grad_stack, preferred_element_type=jnp.float32)
    interior = shards[:, :, 1:-1].reshape(number_rows, rows * cols)
    tap_grads = lax.dot_general(
        source_stack, interior, (((1,), (1,)), ((), ())), preferred_element_type=jnp.float32
    )
    tap_grads = jnp.transpose(tap_grads.reshape(3, 3, cin_dev, number_rows), (2, 0, 1, 3))
    filter_sum = tap_grads
    input_sum, filter_sum = (input_sum, filter_sum)
    filter_total = lax.psum(filter_sum, "width")
    factor = 1.0 / math.sqrt(rows * cols * lax.axis_size("width"))
    input_grad = input_sum.reshape(cin_dev, rows, cols).astype(jnp.bfloat16)
    return (conv_output, input_grad, filter_total * factor)


def solution(mesh):
    in_specs = (P("chan", None, "width"), P("chan", None, None, None), P("chan", None, "width"))
    out_specs = (P("chan", None, "width"), P("chan", None, "width"), P("chan", None, None, None))
    return jax.shard_map(body, mesh=mesh, in_specs=in_specs, out_specs=out_specs, check_vma=False)
```

profile of v0, /device:TPU:8, one launch (start us, length us, event | category | flops | bytes accessed | tf_op | source)
XLA Modules:
  0.0 344.5 jit_solution(17910656039230067917)
XLA Ops:
  7.2 0.0 copy-start.14
  7.2 0.0 copy-start.12
  7.2 0.0 all-gather.2.cloned.1.call-start
  7.2 0.9 fusion.8
  8.1 4.9 %collective-permute-start.2 = (bf16[32,2,1]{2,1,0:T(2,128)(2,1)S(1)}, bf16[32,2,1]{2,1,0:T(2,128)(2,1)S(1)}, u32[]{:S(2)}, u32[]{:S(2)}) collective-permute-start(bf16[32,2,1]{2,1,0:T(2,128)(2,1)S(1)} %get-tuple-element.18), channel_id=1, source_target_pairs={{0,16},{16,32},{32,48},{48,64},{64,80},{80,96},{96,112},{112,128},... | collective-permute-start | bytes 392 | tf_op jit(solution)/shard_map/ppermute | solution.py:15
  13.0 1.3 collective-permute-start.3
  14.3 0.8 fusion.9
  15.2 6.1 %collective-permute-start = (bf16[32,2,1]{2,1,0:T(2,128)(2,1)S(1)}, bf16[32,2,1]{2,1,0:T(2,128)(2,1)S(1)}, u32[]{:S(2)}, u32[]{:S(2)}) collective-permute-start(bf16[32,2,1]{2,1,0:T(2,128)(2,1)S(1)} %get-tuple-element.22), channel_id=1, source_target_pairs={{0,16},{16,32},{32,48},{48,64},{64,80},{80,96},{96,112},{112,128},... | collective-permute-start | bytes 392 | tf_op jit(solution)/shard_map/ppermute | solution.py:15
  21.2 1.3 collective-permute-start.1
  22.5 1.2 copy.10
  23.8 0.4 reshape.94
  24.2 0.6 dynamic-slice
  25.4 0.0 collective-permute-done.2
  25.5 0.0 collective-permute-done.3
  25.5 0.9 pad_maximum_fusion
  26.4 0.0 all-gather.2.cloned.1.call-update
  26.4 0.0 all-reduce.6.cloned.1.call-start
  26.4 0.0 collective-permute-done
  26.4 1.9 collective-permute-done.1
  28.4 0.4 select_maximum_fusion
  28.7 0.6 fusion.7
  29.4 0.0 copy-start.11
  29.4 0.3 pad_maximum_fusion.1
  30.0 0.3 copy-done.11
  30.4 1.0 fusion.10
  31.4 0.0 copy-done.8
  31.4 3.5 %copy.9 = f32[512,2,768]{2,1,0:T(2,128)} copy(f32[512,2,768]{0,2,1:T(8,128)S(1)} %bitcast.58) | data formatting | bytes 6291456 | tf_op jit(solution)/shard_map/reshape | solution.py:55
  34.9 80.9 %all-reduce.7 = bf16[512,2,768]{2,1,0:T(2,128)(2,1)S(1)} all-reduce(f32[512,2,768]{2,1,0:T(2,128)} %copy.9), channel_id=2, replica_groups=mesh['width'=16,'chan'=16] {'chan'}, use_global_device_ids=true, to_apply=%region_0.1.clone | all-reduce | flops 786432 | bytes 4718592
  115.8 0.7 dynamic-slice_convert_fusion
  116.5 33.4 %pad_slice_fusion = (bf16[512,2,768]{2,1,0:T(2,128)(2,1)}, bf16[512,2,768]{2,1,0:T(2,128)(2,1)S(1)}, bf16[512,2,768]{2,1,0:T(2,128)(2,1)S(1)}, bf16[512,2,768]{2...) fusion(bf16[512,2,770]{2,1,0:T(2,128)(2,1)} %all-gather.2.clone, ...), kind=kLoop, calls=%fused_computation | loop fusion | bytes 20709376 | tf_op jit(solution)/shard_map/slice | solution.py:32
  149.9 0.3 copy.21
  150.2 1.3 constant_dynamic-update-slice_fusion.17
  151.4 1.4 copy.22
  152.9 1.4 copy.23
  154.3 1.4 copy.24
  155.7 1.9 reshape.95
  157.6 1.4 copy.25
  159.0 0.5 copy-done.7
  159.5 1.4 copy.26
  160.9 0.5 copy-done.6
  161.4 1.4 copy.27
  162.8 0.3 copy.28
  163.1 1.1 copy-done.5
  164.2 0.3 copy.29
  164.5 0.9 copy-done.9
  165.4 0.5 copy-done.10
  165.9 1.5 fusion.3
  167.4 0.0 all-reduce.6.cloned.1.call-update
  167.4 2.8 constant_dynamic-update-slice_fusion.16
  170.2 1.3 constant_dynamic-update-slice_fusion.15
  171.4 0.7 copy-done.2
  172.2 1.3 constant_dynamic-update-slice_fusion.14
  173.4 0.7 copy-done.3
  174.1 1.2 constant_dynamic-update-slice_fusion.13
  175.4 0.7 copy-done.1
  176.1 1.3 constant_dynamic-update-slice_fusion.12
  177.4 0.6 copy-done
  178.1 1.2 constant_dynamic-update-slice_fusion.11
  179.3 1.3 constant_dynamic-update-slice_fusion.10
  180.6 1.3 constant_dynamic-update-slice_fusion.9
  181.9 7.5 %fusion = bf16[32,1536]{1,0:T(8,128)(2,1)S(1)} fusion(bf16[32,4608]{1,0:T(8,128)(2,1)S(1)} %reshape.94, bf16[4608,1536]{1,0:T(8,128)(2,1)} %constant_dynamic-update-slice_fusion.9), kind=kOutput, calls=%fused_computation.7 | convolution fusion | flops 453033984 | bytes 14548992 | tf_op jit(solution)/shard_map/dot_general | solution.py:66
  189.4 0.7 convert_element_type.19
  190.1 145.6 %all-reduce.6.cloned.1.call-done = f32[32,3,3,512]{3,0,2,1:T(8,128)} async-done(((f32[32,3,3,512]{3,0,2,1:T(8,128)}), f32[32,3,3,512]{3,0,2,1:T(8,128)}) %all-reduce.6.cloned.1.call-update) | async-done | bytes 589840 | tf_op jit(solution)/shard_map/psum | solution.py:74
  335.7 1.9 broadcast_multiply_fusion
  (35 shorter events, 0.2 us)
Async XLA Ops:
  7.2 17.0 %copy-start.14 = (u32[256]{0:T(256)S(1)}, u32[256]{0:T(256)}, u32[]{:S(2)}) copy-start(u32[256]{0:T(256)} %constant.11) | copy-start | bytes 3076
  7.2 18.3 %copy-start.13 = (bf16[32,2,768]{2,1,0:T(2,128)(2,1)S(1)}, bf16[32,2,768]{2,1,0:T(2,128)(2,1)}, u32[]{:S(2)}) copy-start(bf16[32,2,768]{2,1,0:T(2,128)(2,1)} %param.5) | copy-start | bytes 294916
  7.2 17.0 %copy-start.12 = (bf16[32,2,768]{2,1,0:T(2,128)(2,1)S(1)}, bf16[32,2,768]{2,1,0:T(2,128)(2,1)}, u32[]{:S(2)}) copy-start(bf16[32,2,768]{2,1,0:T(2,128)(2,1)} %param.3) | copy-start | bytes 294916
  7.2 109.3 %all-gather.2.cloned.1.call-start = ((), (), s32[]{:S(2)}) async-start(), calls=%async_computation | async-start | bytes 1949696 | tf_op jit(solution)/shard_map/all_gather | solution.py:62
  8.1 17.3 %collective-permute-start.2 = (bf16[32,2,1]{2,1,0:T(2,128)(2,1)S(1)}, bf16[32,2,1]{2,1,0:T(2,128)(2,1)S(1)}, u32[]{:S(2)}, u32[]{:S(2)}) collective-permute-start(bf16[32,2,1]{2,1,0:T(2,128)(2,1)S(1)} %get-tuple-element.18), channel_id=1, source_target_pairs={{0,16},{16,32},{32,48},{48,64},{64,80},{80,96},{96,112},{112,128},... | collective-permute-start | bytes 392 | tf_op jit(solution)/shard_map/ppermute | solution.py:15
  13.0 12.4 %collective-permute-start.3 = (bf16[32,2,1]{2,1,0:T(2,128)(2,1)S(1)}, bf16[32,2,1]{2,1,0:T(2,128)(2,1)S(1)}, u32[]{:S(2)}, u32[]{:S(2)}) collective-permute-start(bf16[32,2,1]{2,1,0:T(2,128)(2,1)S(1)} %get-tuple-element.19), channel_id=1, source_target_pairs={{16,0},{32,16},{48,32},{64,48},{80,64},{96,80},{112,96},{128,112},... | collective-permute-start | bytes 392 | tf_op jit(solution)/shard_map/ppermute | solution.py:16
  15.2 11.3 %collective-permute-start = (bf16[32,2,1]{2,1,0:T(2,128)(2,1)S(1)}, bf16[32,2,1]{2,1,0:T(2,128)(2,1)S(1)}, u32[]{:S(2)}, u32[]{:S(2)}) collective-permute-start(bf16[32,2,1]{2,1,0:T(2,128)(2,1)S(1)} %get-tuple-element.22), channel_id=1, source_target_pairs={{0,16},{16,32},{32,48},{48,64},{64,80},{80,96},{96,112},{112,128},... | collective-permute-start | bytes 392 | tf_op jit(solution)/shard_map/ppermute | solution.py:15
  21.2 7.1 %collective-permute-start.1 = (bf16[32,2,1]{2,1,0:T(2,128)(2,1)S(1)}, bf16[32,2,1]{2,1,0:T(2,128)(2,1)S(1)}, u32[]{:S(2)}, u32[]{:S(2)}) collective-permute-start(bf16[32,2,1]{2,1,0:T(2,128)(2,1)S(1)} %get-tuple-element.23), channel_id=1, source_target_pairs={{16,0},{32,16},{48,32},{64,48},{80,64},{96,80},{112,96},{128,112},... | collective-permute-start | bytes 392 | tf_op jit(solution)/shard_map/ppermute | solution.py:16
  26.4 309.3 %all-reduce.6.cloned.1.call-start = ((), (), s32[]{:S(2)}) async-start(), calls=%async_computation.1 | async-start | bytes 1179648 | tf_op jit(solution)/shard_map/psum | solution.py:74
  29.4 1.0 copy-start.11
  30.0 1.4 copy-start.8
  157.6 1.9 copy-start.7
  159.5 1.9 copy-start.6
  162.8 1.4 copy-start.5
  164.2 1.2 copy-start.9
  164.2 1.7 copy-start.10
  167.4 2.8 copy-start.4
  170.2 2.0 copy-start.2
  172.1 2.0 copy-start.3
  174.1 2.0 copy-start.1
  176.1 2.0 copy-start
Sparse Core Ops, SparseCore 0:
  26.5 44.9 all-gather.1
  167.5 168.1 all-reduce.5
where the time goes:
time: 345 us; the launch traced here: 344 us
  waiting for transfers between devices  148 us (43%)
  blocking collectives  80.9 us (23%)
  local copies, waits for them, and re-layouts  73.8 us (21%)
  between operations  15.1 us (4%)
  starting transfers between devices  13.6 us (4%)
  matrix products  9.99 us (3%)
  other arithmetic  3.53 us (1%)
    psum x1, waiting for transfers between devices, body(): filter_total = lax.psum(filter_sum, 'width')  146 us
    unnamed x1, blocking collectives  80.9 us
    slice x2, local copies, waits for them, and re-layouts, stack_taps(): padded[:, first_row:first_row + rows, first_col:first_col + cols]  34 us
    unnamed x66, local copies, waits for them, and re-layouts  29.6 us
    ppermute x2, starting transfers between devices, padded_2(): before = lax.ppermute(last, axis, up)  11 us
    dot_general x1, matrix products, body(): input_sum = jnp.dot(block, grad_stack, preferred_element_type=jnp.float32)  7.52 us
  transfers between devices with their start and end apart: 6, of which 2 were waited for; matrix products, arithmetic and copies ran while one was open for 9% of the time, Pallas kernels for 0%

commit v1 on v0

--- a/solution.py
+++ b/solution.py
@@ -71,7 +71,7 @@
     tap_grads = jnp.transpose(tap_grads.reshape(3, 3, cin_dev, number_rows), (2, 0, 1, 3))
     filter_sum = tap_grads
     input_sum, filter_sum = (input_sum, filter_sum)
-    filter_total = lax.psum(filter_sum, "width")
+    filter_total = jnp.sum(lax.all_gather(filter_sum, "width"), axis=0)
     factor = 1.0 / math.sqrt(rows * cols * lax.axis_size("width"))
     input_grad = input_sum.reshape(cin_dev, rows, cols).astype(jnp.bfloat16)
     return (conv_output, input_grad, filter_total * factor)

time: 345 us -> 292 us (0.85); the launches traced: 344 us -> 287 us
  waiting for transfers between devices: 148 us -> 87.3 us
  blocking collectives: 80.9 us -> 102 us
  local copies, waits for them, and re-layouts: 73.8 us -> 53.1 us
  other arithmetic: 3.53 us -> 9.12 us
    psum x1 -> x0, waiting for transfers between devices: 146 us -> none  [body(): filter_total = lax.psum(filter_sum, 'width')]
    all_gather x0 -> x1, waiting for transfers between devices: none -> 52.8 us  [body(): filter_total = jnp.sum(lax.all_gather(filter_sum, 'width'), axis=0)]
    all_gather x1, waiting for transfers between devices: 0.01 us -> 23.8 us  [body(): shards = lax.all_gather(grad_edged, 'chan', axis=0, tiled=True)]
    unnamed x1, blocking collectives: 80.9 us -> 102 us
    unnamed x66 -> x64, local copies, waits for them, and re-layouts: 29.6 us -> 10.1 us
    ppermute x2, waiting for transfers between devices: 1.92 us -> 10.6 us  [padded_2(): after = lax.ppermute(leading, axis, down)]
    dot_general x1, matrix products: 7.52 us -> 2.5 us  [body(): input_sum = jnp.dot(block, grad_stack, preferred_element_type=jnp.float32)]
    reduce_sum x0 -> x1, other arithmetic: none -> 4.84 us  [body(): filter_total = jnp.sum(lax.all_gather(filter_sum, 'width'), axis=0)]
  transfers between devices with their start and end apart: 6 -> 6, of which waited for: 2 -> 5; matrix products, arithmetic and copies ran while one was open for 9% -> 6% of each run, Pallas kernels for 0% -> 0%
where the time goes in v1:
time: 292 us; the launch traced here: 287 us
  blocking collectives  102 us (35%)
  waiting for transfers between devices  87.3 us (30%)
  local copies, waits for them, and re-layouts  53.1 us (18%)
  between operations  15.2 us (5%)
  starting transfers between devices  12.3 us (4%)
  other arithmetic  9.12 us (3%)
  matrix products  7.66 us (3%)
    unnamed x1, blocking collectives  102 us
    all_gather x1, waiting for transfers between devices, body(): filter_total = jnp.sum(lax.all_gather(filter_sum, 'width'), axis=0)  52.8 us
    slice x2, local copies, waits for them, and re-layouts, stack_taps(): padded[:, first_row:first_row + rows, first_col:first_col + cols]  33.9 us
    all_gather x1, waiting for transfers between devices, body(): shards = lax.all_gather(grad_edged, 'chan', axis=0, tiled=True)  23.8 us
    ppermute x2, waiting for transfers between devices, padded_2(): after = lax.ppermute(leading, axis, down)  10.6 us
    unnamed x64, local copies, waits for them, and re-layouts  10.1 us
    ppermute x2, starting transfers between devices, padded_2(): before = lax.ppermute(last, axis, up)  9.6 us
  transfers between devices with their start and end apart: 6, of which 5 were waited for; matrix products, arithmetic and copies ran while one was open for 6% of the time, Pallas kernels for 0%

profile of v1, /device:TPU:8, one launch (start us, length us, event | category | flops | bytes accessed | tf_op | source)
XLA Modules:
  0.0 287.1 jit_solution(6758565142396160245)
XLA Ops:
  7.2 0.0 copy-start.12
  7.2 0.0 all-gather.4.cloned.1.call-start
  7.2 0.8 fusion.8
  8.1 4.9 %collective-permute-start.2 = (bf16[32,2,1]{2,1,0:T(2,128)(2,1)S(1)}, bf16[32,2,1]{2,1,0:T(2,128)(2,1)S(1)}, u32[]{:S(2)}, u32[]{:S(2)}) collective-permute-start(bf16[32,2,1]{2,1,0:T(2,128)(2,1)S(1)} %get-tuple-element.18), channel_id=1, source_target_pairs={{0,16},{16,32},{32,48},{48,64},{64,80},{80,96},{96,112},{112,128},... | collective-permute-start | bytes 392 | tf_op jit(solution)/shard_map/ppermute | solution.py:15
  13.0 1.3 collective-permute-start.3
  14.3 0.1 collective-permute-done.2
  14.4 5.7 %collective-permute-done.3 = bf16[32,2,1]{2,1,0:T(2,128)(2,1)S(1)} collective-permute-done((bf16[32,2,1]{2,1,0:T(2,128)(2,1)S(1)}, bf16[32,2,1]{2,1,0:T(2,128)(2,1)S(1)}, u32[]{:S(2)}, u32[]{:S(2)}) %collective-permute-start.3) | collective-permute-done | bytes 160 | tf_op jit(solution)/shard_map/ppermute | solution.py:16
  20.1 1.8 pad_maximum_fusion
  21.9 0.0 all-gather.4.cloned.1.call-update
  21.9 0.0 all-gather.6.cloned.1.call-start
  22.0 0.8 fusion.9
  22.8 4.7 %collective-permute-start = (bf16[32,2,1]{2,1,0:T(2,128)(2,1)S(1)}, bf16[32,2,1]{2,1,0:T(2,128)(2,1)S(1)}, u32[]{:S(2)}, u32[]{:S(2)}) collective-permute-start(bf16[32,2,1]{2,1,0:T(2,128)(2,1)S(1)} %get-tuple-element.22), channel_id=1, source_target_pairs={{0,16},{16,32},{32,48},{48,64},{64,80},{80,96},{96,112},{112,128},... | collective-permute-start | bytes 392 | tf_op jit(solution)/shard_map/ppermute | solution.py:15
  27.5 1.3 collective-permute-start.1
  28.8 0.9 copy.16
  29.7 0.0 collective-permute-done
  29.7 4.9 %collective-permute-done.1 = bf16[32,2,1]{2,1,0:T(2,128)(2,1)S(1)} collective-permute-done((bf16[32,2,1]{2,1,0:T(2,128)(2,1)S(1)}, bf16[32,2,1]{2,1,0:T(2,128)(2,1)S(1)}, u32[]{:S(2)}, u32[]{:S(2)}) %collective-permute-start.1) | collective-permute-done | bytes 160 | tf_op jit(solution)/shard_map/ppermute | solution.py:16
  34.6 1.3 select_maximum_fusion
  35.9 0.6 fusion.7
  36.6 0.3 pad_maximum_fusion.1
  37.2 0.0 copy-start.10
  37.2 23.8 %all-gather.4.cloned.1.call-done = bf16[512,2,770]{2,1,0:T(2,128)(2,1)} async-done(((bf16[32,2,770]{2,1,0:T(2,128)(2,1)}), bf16[512,2,770]{2,1,0:T(2,128)(2,1)}) %all-gather.4.cloned.1.call-update) | async-done | bytes 1576976 | tf_op jit(solution)/shard_map/all_gather | solution.py:62
  60.9 33.3 %pad_slice_fusion = (bf16[512,2,768]{2,1,0:T(2,128)(2,1)}, bf16[512,2,768]{2,1,0:T(2,128)(2,1)}, bf16[512,2,768]{2,1,0:T(2,128)(2,1)}, bf16[512,2,768]{2,1,0:T(2...) fusion(bf16[512,2,770]{2,1,0:T(2,128)(2,1)} %all-gather.4.clone, ...), kind=kLoop, calls=%fused_computation | loop fusion | bytes 20709376 | tf_op jit(solution)/shard_map/slice | solution.py:32
  94.3 2.0 reshape.96
  96.2 2.9 %fusion.3 = f32[32,3,3,512]{3,0,2,1:T(8,128)} fusion(bf16[3,3,32,1536]{3,2,1,0:T(8,128)(2,1)S(1)} %bitcast.79, bf16[512,1536,1,1]{1,0,2,3:T(8,128)(2,1)} %reshape.96), kind=kOutput, calls=%fused_computation.10 | convolution fusion | flops 452984832 | bytes 3047424 | tf_op jit(solution)/shard_map/dot_general | solution.py:68
  99.2 0.0 all-gather.6.cloned.1.call-update
  99.2 0.3 copy.10
  99.5 0.4 reshape.94
  99.9 0.6 dynamic-slice
  101.1 2.2 fusion.10
  103.4 3.6 %copy.9 = f32[512,2,768]{2,1,0:T(2,128)} copy(f32[512,2,768]{0,2,1:T(8,128)S(1)} %bitcast.59) | data formatting | bytes 6291456 | tf_op jit(solution)/shard_map/reshape | solution.py:55
  107.0 102.5 %all-reduce.4 = bf16[512,2,768]{2,1,0:T(2,128)(2,1)S(1)} all-reduce(f32[512,2,768]{2,1,0:T(2,128)} %copy.9), channel_id=3, replica_groups=mesh['width'=16,'chan'=16] {'chan'}, use_global_device_ids=true, to_apply=%region_0.1.clone | all-reduce | flops 786432 | bytes 4718592
  209.4 0.0 copy-start.8
  209.5 0.7 dynamic-slice_convert_fusion
  210.2 0.3 copy.21
  210.4 0.4 copy-done.8
  210.9 0.3 copy.22
  211.2 0.8 copy-done.7
  212.0 0.3 copy.23
  212.2 0.5 copy-done.6
  212.7 0.3 copy.24
  212.9 0.8 copy-done.1
  213.7 0.3 copy.25
  214.0 0.5 copy-done.5
  214.5 0.3 copy.26
  214.8 0.8 copy-done.4
  215.5 0.3 copy.27
  215.8 0.5 copy-done.3
  216.3 0.3 copy.28
  216.5 0.8 copy-done.2
  217.3 0.3 copy.29
  217.6 0.1 constant_dynamic-update-slice_fusion.17
  217.7 0.1 constant_dynamic-update-slice_fusion.16
  217.8 0.1 constant_dynamic-update-slice_fusion.15
  217.9 0.1 constant_dynamic-update-slice_fusion.14
  218.0 0.1 constant_dynamic-update-slice_fusion.13
  218.1 0.1 constant_dynamic-update-slice_fusion.12
  218.2 0.1 constant_dynamic-update-slice_fusion.11
  218.4 0.1 constant_dynamic-update-slice_fusion.10
  218.5 0.1 constant_dynamic-update-slice_fusion.9
  218.6 2.5 fusion
  221.1 0.7 convert_element_type.19
  221.8 52.8 %all-gather.6.cloned.1.call-done = f32[512,3,3,512]{3,0,2,1:T(8,128)} async-done(((f32[32,3,3,512]{3,0,2,1:T(8,128)}), f32[512,3,3,512]{3,0,2,1:T(8,128)}) %all-gather.6.cloned.1.call-update) | async-done | bytes 9437200 | tf_op jit(solution)/shard_map/all_gather | solution.py:74
  274.5 4.8 %reduce_sum.9 = f32[32,3,3,512]{3,0,2,1:T(8,128)S(1)} reduce(f32[16,32,3,3,512]{4,1,0,3,2:T(8,128)} %bitcast.61, f32[]{:T(128)} %constant.2.clone.1), dimensions={0}, to_apply=%region_1.2 | reduce | flops 2211840 | bytes 10027012 | tf_op jit(solution)/shard_map/reduce_sum | solution.py:74
  279.4 0.9 broadcast_multiply_fusion
  (34 shorter events, 0.2 us)
Async XLA Ops:
  7.2 29.4 %copy-start.12 = (bf16[32,2,768]{2,1,0:T(2,128)(2,1)S(1)}, bf16[32,2,768]{2,1,0:T(2,128)(2,1)}, u32[]{:S(2)}) copy-start(bf16[32,2,768]{2,1,0:T(2,128)(2,1)} %param.3) | copy-start | bytes 294916
  7.2 53.8 %all-gather.4.cloned.1.call-start = ((), (), s32[]{:S(2)}) async-start(), calls=%async_computation | async-start | bytes 1949696 | tf_op jit(solution)/shard_map/all_gather | solution.py:62
  8.1 6.4 %collective-permute-start.2 = (bf16[32,2,1]{2,1,0:T(2,128)(2,1)S(1)}, bf16[32,2,1]{2,1,0:T(2,128)(2,1)S(1)}, u32[]{:S(2)}, u32[]{:S(2)}) collective-permute-start(bf16[32,2,1]{2,1,0:T(2,128)(2,1)S(1)} %get-tuple-element.18), channel_id=1, source_target_pairs={{0,16},{16,32},{32,48},{48,64},{64,80},{80,96},{96,112},{112,128},... | collective-permute-start | bytes 392 | tf_op jit(solution)/shard_map/ppermute | solution.py:15
  13.0 7.1 %collective-permute-start.3 = (bf16[32,2,1]{2,1,0:T(2,128)(2,1)S(1)}, bf16[32,2,1]{2,1,0:T(2,128)(2,1)S(1)}, u32[]{:S(2)}, u32[]{:S(2)}) collective-permute-start(bf16[32,2,1]{2,1,0:T(2,128)(2,1)S(1)} %get-tuple-element.19), channel_id=1, source_target_pairs={{16,0},{32,16},{48,32},{64,48},{80,64},{96,80},{112,96},{128,112},... | collective-permute-start | bytes 392 | tf_op jit(solution)/shard_map/ppermute | solution.py:16
  21.9 252.6 %all-gather.6.cloned.1.call-start = ((), (), s32[]{:S(2)}) async-start(), calls=%async_computation.1 | async-start | bytes 10027008 | tf_op jit(solution)/shard_map/all_gather | solution.py:74
  22.8 6.9 %collective-permute-start = (bf16[32,2,1]{2,1,0:T(2,128)(2,1)S(1)}, bf16[32,2,1]{2,1,0:T(2,128)(2,1)S(1)}, u32[]{:S(2)}, u32[]{:S(2)}) collective-permute-start(bf16[32,2,1]{2,1,0:T(2,128)(2,1)S(1)} %get-tuple-element.22), channel_id=1, source_target_pairs={{0,16},{16,32},{32,48},{48,64},{64,80},{80,96},{96,112},{112,128},... | collective-permute-start | bytes 392 | tf_op jit(solution)/shard_map/ppermute | solution.py:15
  27.5 7.1 %collective-permute-start.1 = (bf16[32,2,1]{2,1,0:T(2,128)(2,1)S(1)}, bf16[32,2,1]{2,1,0:T(2,128)(2,1)S(1)}, u32[]{:S(2)}, u32[]{:S(2)}) collective-permute-start(bf16[32,2,1]{2,1,0:T(2,128)(2,1)S(1)} %get-tuple-element.23), channel_id=1, source_target_pairs={{16,0},{32,16},{48,32},{64,48},{80,64},{96,80},{112,96},{128,112},... | collective-permute-start | bytes 392 | tf_op jit(solution)/shard_map/ppermute | solution.py:16
  37.2 59.1 %copy-start.10 = (bf16[288,1536]{1,0:T(8,128)(2,1)}, bf16[288,1536]{1,0:T(8,128)(2,1)S(1)}, u32[]{:S(2)}) copy-start(bf16[288,1536]{1,0:T(8,128)(2,1)S(1)} %constant_dynamic-update-slice_fusion) | copy-start | bytes 2654212
  94.3 4.9 %copy-start = (bf16[512,2,768]{2,1,0:T(2,128)(2,1)}, bf16[512,2,768]{2,1,0:T(2,128)(2,1)S(1)}, u32[]{:S(2)}) copy-start(bf16[512,2,768]{2,1,0:T(2,128)(2,1)S(1)} %get-tuple-element.9) | copy-start | bytes 4718596
  96.2 3.0 %copy-start.11 = (bf16[32,3,3,512]{3,0,2,1:T(8,128)(2,1)S(1)}, bf16[32,3,3,512]{3,0,2,1:T(8,128)(2,1)}, u32[]{:S(2)}) copy-start(bf16[32,3,3,512]{3,0,2,1:T(8,128)(2,1)} %param.4) | copy-start | bytes 884740
  96.2 3.6 %copy-start.13 = (u32[256]{0:T(256)S(1)}, u32[256]{0:T(256)}, u32[]{:S(2)}) copy-start(u32[256]{0:T(256)} %constant.13) | copy-start | bytes 3076
  107.0 103.2 %copy-start.9 = (bf16[512,2,768]{2,1,0:T(2,128)(2,1)S(1)}, bf16[512,2,768]{2,1,0:T(2,128)(2,1)}, u32[]{:S(2)}) copy-start(bf16[512,2,768]{2,1,0:T(2,128)(2,1)} %get-tuple-element.11) | copy-start | bytes 4718596
  209.4 1.4 copy-start.8
  210.4 1.5 copy-start.7
  211.1 1.5 copy-start.6
  212.2 1.5 copy-start.1
  212.9 1.6 copy-start.5
  214.0 1.5 copy-start.4
  214.8 1.5 copy-start.3
  215.8 1.5 copy-start.2
Sparse Core Ops, SparseCore 0:
  22.0 38.8 all-gather.3
  99.3 175.1 all-gather.5
